TPU v7x, 128 devices: a whole 4x4x4 slice. The times are simulated.
128 devices in a mesh: pair: 2 (over x_hi), gx: 8 (over y, x_lo), gy: 8 (over z, core).
Axes of the slice: x: 4 (x_hi: 2, x_lo: 2; x = x_hi * 2 + x_lo), y: 4, z: 4, core: 2. Of those that a mesh axis runs over, the one named last changes fastest.
Arguments:
- sound_speed_sq: float32 [64, 64, 1024], P('gx', 'gy'), may hold values from 0.5 to 2
- wind_profile: float32 [3, 1024], replicated, may hold values from -0.6 to 0.6
- forward_field: bfloat16 [4, 4, 64, 64, 1024], P(None, None, 'gx', 'gy'), may hold values from -6 to 6
- adjoint_state: float32 [2, 4, 64, 64, 1024], P('pair', None, 'gx', 'gy'), may hold values from -0.3125 to 0.3125
- pair_counts: int32 [2], P('pair'), may hold values from 64 to 256, as said below
- source_cells: int32 [512, 3], P('pair'), may hold values from 0 to 1023, as said below
- receiver_cells: int32 [512, 3], P('pair'), may hold values from 0 to 1023, as said below
- residuals: float32 [512, 4], P('pair'), may hold values from -16 to 16
Outputs:
- kernels: float32 [4, 64, 64, 1024], P(None, 'gx', 'gy', 'pair')
- final_state: float32 [2, 4, 64, 64, 1024], P('pair', None, 'gx', 'gy')
Inputs may be any that keep to these rules, and one draw needn't show every extreme that they name: `pair_counts`: one group in every draw has exactly 256 live pairs. `source_cells`: columns are the cell along the first, second and third dimension, each within the grid. `receiver_cells`: columns are the cell along the first, second and third dimension, each within the grid; several pairs may share a cell.
All inputs are finite; a program needn't handle non-finite values.
Results may differ from a plain program's by a relative error of at most 0.00115.
Values may be sent and summed in bfloat16 or wider, within the bound.
A program may use at most 128 MiB of HBM per device.

v0:
```python
import jax
import jax.numpy as jnp
from jax import lax
from jax.sharding import PartitionSpec as P

step_length = 0.25


def extended(shard, sides, width):
    for axis, dim in sides:
        size, length = (lax.axis_size(axis), shard.shape[dim])
        up = [(i, (i + 1) % size) for i in range(size - 1)]
        down = [(j, i) for i, j in up]
        last = lax.slice_in_dim(shard, length - width, length, axis=dim)
        initial = lax.slice_in_dim(shard, 0, width, axis=dim)
        before = lax.ppermute(last, axis, up)
        after = lax.ppermute(initial, axis, down)
        shard = jnp.concatenate([before, shard, after], axis=dim)
    return shard


def central(padded):
    dims = padded.ndim
    east_diff = (padded[..., 2:, 1:-1, :] - padded[..., :-2, 1:-1, :]) * 0.5
    north_diff = (padded[..., 1:-1, 2:, :] - padded[..., 1:-1, :-2, :]) * 0.5
    center = padded[..., 1:-1, 1:-1, :]
    vertical = jnp.pad(center, [(0, 0)] * (dims - 1) + [(1, 1)])
    up_diff = (vertical[..., 2:] - vertical[..., :-2]) * 0.5
    return (east_diff, north_diff, up_diff, center)


def local_flat(cells, width_x, width_y, depth):
    local_x = cells[:, 0] - lax.axis_index("gx") * width_x
    local_y = cells[:, 1] - lax.axis_index("gy") * width_y
    inside = (local_x >= 0) & (local_x < width_x) & (local_y >= 0) & (local_y < width_y)
    flat = (
        jnp.clip(local_x, 0, width_x - 1) * width_y + jnp.clip(local_y, 0, width_y - 1)
    ) * depth + cells[:, 2]
    return (flat, inside.astype(jnp.float32))


def shards(
    sound_speed_sq,
    wind_profile,
    forward_field,
    adjoint_state,
    pair_counts,
    source_cells,
    receiver_cells,
    residuals,
):
    steps_total = forward_field.shape[0]
    width_x, width_y, depth = sound_speed_sq.shape
    slots = residuals.shape[0]
    east_wind = wind_profile[0]
    north_wind = wind_profile[1]
    vertical_wind = wind_profile[2]
    live = (jnp.arange(slots, dtype=jnp.int32) < pair_counts[0]).astype(jnp.float32)
    src_flat, src_inside = local_flat(source_cells, width_x, width_y, depth)
    rcv_flat, rcv_inside = local_flat(receiver_cells, width_x, width_y, depth)
    pressure_snaps = forward_field[:, 0].reshape(steps_total, -1)
    local_samples = (
        jnp.take(pressure_snaps, src_flat, axis=1).astype(jnp.float32) * src_inside[None, :]
    )
    samples = lax.psum(local_samples, ("gx", "gy"))
    state = adjoint_state[0]
    kernel_local = jnp.zeros((4, width_x, width_y, depth), jnp.float32)
    for step in range(steps_total):
        snap = steps_total - 1 - step
        amplitude = residuals[:, snap] * samples[snap] * live * rcv_inside
        injected = (
            jnp.zeros((width_x * width_y * depth,), jnp.float32)
            .at[rcv_flat]
            .add(amplitude)
            .reshape(width_x, width_y, depth)
        )
        padded = extended(state, (("gx", 1), ("gy", 2)), 1)
        east_diff, north_diff, up_diff, center = central(padded)
        pressure = center[0]
        velocity = center[1:]
        divergence = east_diff[1] + north_diff[2] + up_diff[3]
        p_new = (
            pressure
            + step_length
            * (
                sound_speed_sq * divergence
                + east_wind * east_diff[0]
                + north_wind * north_diff[0]
                + vertical_wind * up_diff[0]
            )
            + injected
        )
        p_padded = extended(p_new, (("gx", 0), ("gy", 1)), 1)
        p_east, p_north, p_up, unused_center = central(p_padded)
        gradient = jnp.stack([p_east, p_north, p_up])
        a_new = velocity + step_length * (
            gradient
            + east_wind * east_diff[1:]
            + north_wind * north_diff[1:]
            + vertical_wind * up_diff[1:]
        )
        forward_rim = extended(forward_field[snap], (("gx", 1), ("gy", 2)), 1).astype(jnp.float32)
        f_east, f_north, f_up, unused_forward = central(forward_rim)
        pieces = [p_new * (f_east[1] + f_north[2] + f_up[3])]
        for along in (f_east, f_north, f_up):
            pieces.append(
                p_new * along[0] + a_new[0] * along[1] + a_new[1] * along[2] + a_new[2] * along[3]
            )
        increment = jnp.stack(pieces)
        kernel_local = kernel_local + increment
        state = jnp.concatenate([p_new[None], a_new], axis=0)
    kernels = lax.psum_scatter(kernel_local, "pair", scatter_dimension=3, tiled=True)
    return (kernels, state[None])


def solution(mesh):
    in_specs = (
        P("gx", "gy", None),
        P(),
        P(None, None, "gx", "gy", None),
        P("pair", None, "gx", "gy", None),
        P("pair"),
        P("pair", None),
        P("pair", None),
        P("pair", None),
    )
    out_specs = (P(None, "gx", "gy", "pair"), P("pair", None, "gx", "gy", None))
    return jax.shard_map(shards, mesh=mesh, in_specs=in_specs, out_specs=out_specs, check_vma=False)
```

profile of v0, /device:TPU:1, one launch (start us, length us, event | category | flops | bytes accessed | tf_op | source)
XLA Modules:
  0.0 556.1 jit_solution(320897750737244086)
XLA Ops:
  7.2 1.8 slice_bitcast_fusion
  11.0 5.2 collective-permute-start.4
  17.0 3.7 collective-permute-start.1
  20.6 1.3 collective-permute-start
  23.9 1.9 slice.831
  26.9 13.0 %copy.11 = bf16[4,1,8,8,1024]{0,4,3,2,1:T(8,128)(2,1)} copy(bf16[4,1,8,8,1024]{4,3,2,1,0:T(8,128)(2,1)} %slice.831) | data formatting | bytes 1048576 | tf_op jit(solution)/shard_map/slice | solution.py:61
  40.0 8.7 %gather_fusion = bf16[256,4]{1,0:T(8,128)(2,1)S(1)} fusion(bf16[4,65536]{0,1:T(8,128)(2,1)} %bitcast.532, s32[1024]{0:T(1024)S(1)} %pad_clamp_fusion), kind=kCustom, calls=%fused_computation | custom fusion | bytes 5120 | tf_op jit(solution)/shard_map/jit(_take)/gather | solution.py:63
  48.8 278.8 %psum.7 = f32[4,256]{0,1:T(8,128)S(1)} all-reduce(f32[4,256]{0,1:T(8,128)S(1)} %multiply_bitcast_fusion), channel_id=1, replica_groups=mesh['pair'=2,'gx'=8,'gy'=8] {'gx','gy'}, use_global_device_ids=true, to_apply=%region_0.1 | all-reduce | flops 1024 | bytes 8192 | tf_op jit(solution)/shard_map/psum | solution.py:65
  332.6 2.2 scatter_custom_fusion
  335.5 2.2 scatter_custom_fusion.1
  338.5 2.2 scatter_custom_fusion.2
  341.4 2.8 scatter_custom_fusion.3
  345.2 1.3 collective-permute-start.16
  349.0 4.0 collective-permute-start.28
  355.5 4.0 collective-permute-start.40
  359.5 9.9 %collective-permute-start.7 = (bf16[4,10,1,1024]{3,2,1,0:T(2,128)(2,1)S(1)}, bf16[4,10,1,1024]{3,2,1,0:T(2,128)(2,1)S(1)}, u32[]{:S(2)}, u32[]{:S(2)}) collective-permute-start(bf16[4,10,1,1024]{3,2,1,0:T(2,128)(2,1)S(1)} %get-tuple-element.75), channel_id=1, source_target_pairs={{1,0},{2,1},{3,2},{4,3},{5,4},{6,5},{7,6},{9,8},{10,9},{11,10},{12... | collective-permute-start | bytes 245768 | tf_op jit(solution)/shard_map/ppermute | solution.py:17
  369.6 1.9 collective-permute-start.6
  371.5 2.4 collective-permute-start.19
  374.2 3.2 collective-permute-start.18
  377.3 1.9 collective-permute-start.31
  380.5 3.6 collective-permute-start.3
  384.1 2.1 collective-permute-start.2
  386.2 1.6 maximum_convert_fusion
  389.1 3.8 collective-permute-start.30
  392.9 1.9 collective-permute-start.43
  394.8 1.9 fusion.39
  397.1 2.5 collective-permute-start.9
  400.9 1.5 maximum_convert_fusion.1
  402.5 1.8 collective-permute-done.8
  404.4 5.1 collective-permute-start.11
  409.4 1.9 collective-permute-start.10
  412.0 2.8 collective-permute-done.10
  415.5 2.5 collective-permute-start.13
  420.0 2.7 collective-permute-start.42
  423.9 3.3 collective-permute-start.15
  427.3 1.9 collective-permute-start.14
  429.9 4.0 collective-permute-done.14
  435.4 2.5 collective-permute-start.21
  439.9 2.7 collective-permute-done.20
  442.6 3.2 collective-permute-start.23
  445.8 1.9 collective-permute-start.22
  448.5 2.7 collective-permute-done.22
  451.9 2.5 collective-permute-start.25
  456.3 3.8 collective-permute-done.24
  460.3 3.3 collective-permute-start.27
  463.7 2.1 collective-permute-start.26
  467.1 3.2 collective-permute-done.26
  471.8 2.6 collective-permute-start.33
  476.0 3.0 collective-permute-done.32
  479.1 3.2 collective-permute-start.35
  482.3 1.9 collective-permute-start.34
  484.4 3.2 collective-permute-done.34
  488.3 2.5 collective-permute-start.37
  492.8 3.8 collective-permute-done.36
  496.8 4.3 collective-permute-start.39
  501.1 1.9 collective-permute-start.38
  503.3 4.4 collective-permute-done.38
  509.2 2.2 collective-permute-start.45
  513.1 3.0 collective-permute-done.44
  516.1 3.2 collective-permute-start.47
  519.3 1.9 collective-permute-start.46
  521.4 3.2 collective-permute-done.46
  525.8 1.5 fusion.41
  528.4 20.9 %reduce-scatter.2.cloned.1.call-done = f32[4,8,8,512]{3,2,1,0:T(8,128)} async-done(((f32[4,8,8,1024]{3,2,1,0:T(8,128)}), f32[4,8,8,512]{3,2,1,0:T(8,128)}) %reduce-scatter.2.cloned.1.call-update) | async-done | bytes 524304 | tf_op jit(solution)/shard_map/reduce_scatter | solution.py:112
  (138 shorter events, 48.2 us)
Async XLA Ops:
  7.2 9.1 %copy-start = (f32[1,4,8,8,1024]{4,3,2,1,0:T(8,128)S(1)}, f32[1,4,8,8,1024]{4,3,2,1,0:T(8,128)}, u32[]{:S(2)}) copy-start(f32[1,4,8,8,1024]{4,3,2,1,0:T(8,128)} %param.11) | copy-start | bytes 3145732
  7.2 18.6 %copy-start.6 = (f32[256,4]{0,1:T(4,128)S(1)}, f32[256,4]{0,1:T(4,128)}, u32[]{:S(2)}) copy-start(f32[256,4]{0,1:T(4,128)} %param.15) | copy-start | bytes 12292
  7.2 19.2 %copy-start.5 = (s32[256,3]{0,1:T(4,128)S(1)}, s32[256,3]{0,1:T(4,128)}, u32[]{:S(2)}) copy-start(s32[256,3]{0,1:T(4,128)} %param.14) | copy-start | bytes 9220
  7.2 19.7 %copy-start.7 = (s32[256,3]{0,1:T(4,128)S(1)}, s32[256,3]{0,1:T(4,128)}, u32[]{:S(2)}) copy-start(s32[256,3]{0,1:T(4,128)} %param.13) | copy-start | bytes 9220
  7.2 542.1 %reduce-scatter.2.cloned.1.call-start = ((), (), s32[]{:S(2)}) async-start(), calls=%async_computation.1 | async-start | bytes 1572864 | tf_op jit(solution)/shard_map/reduce_scatter | solution.py:112
  9.7 335.5 %collective-permute-start.5 = (bf16[4,1,8,1024]{3,2,1,0:T(8,128)(2,1)}, bf16[4,1,8,1024]{3,2,1,0:T(8,128)(2,1)}, u32[]{:S(2)}, u32[]{:S(2)}) collective-permute-start(bf16[4,1,8,1024]{3,2,1,0:T(8,128)(2,1)} %get-tuple-element.83), channel_id=1, source_target_pairs={{8,0},{16,8},{24,16},{32,24},{40,32},{48,40},{56,48},{9,1},{17,9},... | collective-permute-start | bytes 196616 | tf_op jit(solution)/shard_map/ppermute | solution.py:17
  11.0 335.5 %collective-permute-start.4 = (bf16[4,1,8,1024]{3,2,1,0:T(8,128)(2,1)}, bf16[4,1,8,1024]{3,2,1,0:T(8,128)(2,1)}, u32[]{:S(2)}, u32[]{:S(2)}) collective-permute-start(bf16[4,1,8,1024]{3,2,1,0:T(8,128)(2,1)} %get-tuple-element.82), channel_id=1, source_target_pairs={{0,8},{8,16},{16,24},{24,32},{32,40},{40,48},{48,56},{1,9},{9,17},... | collective-permute-start | bytes 196616 | tf_op jit(solution)/shard_map/ppermute | solution.py:16
  17.0 357.2 %collective-permute-start.1 = (f32[4,1,8,1024]{3,2,1,0:T(8,128)}, f32[4,1,8,1024]{3,2,1,0:T(8,128)S(1)}, u32[]{:S(2)}, u32[]{:S(2)}) collective-permute-start(f32[4,1,8,1024]{3,2,1,0:T(8,128)} %get-tuple-element.66), channel_id=1, source_target_pairs={{0,8},{8,16},{16,24},{24,32},{32,40},{40,48},{48,56},{1,9},{9,17},... | collective-permute-start | bytes 393224 | tf_op jit(solution)/shard_map/ppermute | solution.py:16
  20.6 356.7 %collective-permute-start = (f32[4,1,8,1024]{3,2,1,0:T(8,128)}, f32[4,1,8,1024]{3,2,1,0:T(8,128)}, u32[]{:S(2)}, u32[]{:S(2)}) collective-permute-start(f32[4,1,8,1024]{3,2,1,0:T(8,128)} %get-tuple-element.67), channel_id=1, source_target_pairs={{8,0},{16,8},{24,16},{32,24},{40,32},{48,40},{56,48},{9,1},{17,9},... | collective-permute-start | bytes 393224 | tf_op jit(solution)/shard_map/ppermute | solution.py:17
  22.6 326.4 %collective-permute-start.17 = (bf16[4,1,8,1024]{3,2,1,0:T(8,128)(2,1)}, bf16[4,1,8,1024]{3,2,1,0:T(8,128)(2,1)}, u32[]{:S(2)}, u32[]{:S(2)}) collective-permute-start(bf16[4,1,8,1024]{3,2,1,0:T(8,128)(2,1)} %get-tuple-element.81), channel_id=1, source_target_pairs={{8,0},{16,8},{24,16},{32,24},{40,32},{48,40},{56,48},{9,1},{17,9},... | collective-permute-start | bytes 196616 | tf_op jit(solution)/shard_map/ppermute | solution.py:17
  345.2 7.8 %collective-permute-start.16 = (bf16[4,1,8,1024]{3,2,1,0:T(8,128)(2,1)}, bf16[4,1,8,1024]{3,2,1,0:T(8,128)(2,1)S(1)}, u32[]{:S(2)}, u32[]{:S(2)}) collective-permute-start(bf16[4,1,8,1024]{3,2,1,0:T(8,128)(2,1)} %get-tuple-element.80), channel_id=1, source_target_pairs={{0,8},{8,16},{16,24},{24,32},{32,40},{40,48},{48,56},{1,9},{9,17},... | collective-permute-start | bytes 196616 | tf_op jit(solution)/shard_map/ppermute | solution.py:16
  346.5 8.9 %collective-permute-start.29 = (bf16[4,1,8,1024]{3,2,1,0:T(8,128)(2,1)}, bf16[4,1,8,1024]{3,2,1,0:T(8,128)(2,1)S(1)}, u32[]{:S(2)}, u32[]{:S(2)}) collective-permute-start(bf16[4,1,8,1024]{3,2,1,0:T(8,128)(2,1)} %get-tuple-element.79), channel_id=1, source_target_pairs={{8,0},{16,8},{24,16},{32,24},{40,32},{48,40},{56,48},{9,1},{17,9},... | collective-permute-start | bytes 196616 | tf_op jit(solution)/shard_map/ppermute | solution.py:17
  349.0 10.5 %collective-permute-start.28 = (bf16[4,1,8,1024]{3,2,1,0:T(8,128)(2,1)}, bf16[4,1,8,1024]{3,2,1,0:T(8,128)(2,1)S(1)}, u32[]{:S(2)}, u32[]{:S(2)}) collective-permute-start(bf16[4,1,8,1024]{3,2,1,0:T(8,128)(2,1)} %get-tuple-element.78), channel_id=1, source_target_pairs={{0,8},{8,16},{16,24},{24,32},{32,40},{40,48},{48,56},{1,9},{9,17},... | collective-permute-start | bytes 196616 | tf_op jit(solution)/shard_map/ppermute | solution.py:16
  353.0 16.6 %collective-permute-start.41 = (bf16[4,1,8,1024]{3,2,1,0:T(8,128)(2,1)}, bf16[4,1,8,1024]{3,2,1,0:T(8,128)(2,1)S(1)}, u32[]{:S(2)}, u32[]{:S(2)}) collective-permute-start(bf16[4,1,8,1024]{3,2,1,0:T(8,128)(2,1)} %get-tuple-element.77), channel_id=1, source_target_pairs={{8,0},{16,8},{24,16},{32,24},{40,32},{48,40},{56,48},{9,1},{17,9},... | collective-permute-start | bytes 196616 | tf_op jit(solution)/shard_map/ppermute | solution.py:17
  355.5 16.0 %collective-permute-start.40 = (bf16[4,1,8,1024]{3,2,1,0:T(8,128)(2,1)}, bf16[4,1,8,1024]{3,2,1,0:T(8,128)(2,1)S(1)}, u32[]{:S(2)}, u32[]{:S(2)}) collective-permute-start(bf16[4,1,8,1024]{3,2,1,0:T(8,128)(2,1)} %get-tuple-element.76), channel_id=1, source_target_pairs={{0,8},{8,16},{16,24},{24,32},{32,40},{40,48},{48,56},{1,9},{9,17},... | collective-permute-start | bytes 196616 | tf_op jit(solution)/shard_map/ppermute | solution.py:16
  359.5 21.0 %collective-permute-start.7 = (bf16[4,10,1,1024]{3,2,1,0:T(2,128)(2,1)S(1)}, bf16[4,10,1,1024]{3,2,1,0:T(2,128)(2,1)S(1)}, u32[]{:S(2)}, u32[]{:S(2)}) collective-permute-start(bf16[4,10,1,1024]{3,2,1,0:T(2,128)(2,1)S(1)} %get-tuple-element.75), channel_id=1, source_target_pairs={{1,0},{2,1},{3,2},{4,3},{5,4},{6,5},{7,6},{9,8},{10,9},{11,10},{12... | collective-permute-start | bytes 245768 | tf_op jit(solution)/shard_map/ppermute | solution.py:17
  369.6 14.5 %collective-permute-start.6 = (bf16[4,10,1,1024]{3,2,1,0:T(2,128)(2,1)S(1)}, bf16[4,10,1,1024]{3,2,1,0:T(2,128)(2,1)S(1)}, u32[]{:S(2)}, u32[]{:S(2)}) collective-permute-start(bf16[4,10,1,1024]{3,2,1,0:T(2,128)(2,1)S(1)} %get-tuple-element.74), channel_id=1, source_target_pairs={{0,1},{1,2},{2,3},{3,4},{4,5},{5,6},{6,7},{8,9},{9,10},{10,11},{11... | collective-permute-start | bytes 245768 | tf_op jit(solution)/shard_map/ppermute | solution.py:16
  371.5 25.6 %collective-permute-start.19 = (bf16[4,10,1,1024]{3,2,1,0:T(2,128)(2,1)S(1)}, bf16[4,10,1,1024]{3,2,1,0:T(2,128)(2,1)S(1)}, u32[]{:S(2)}, u32[]{:S(2)}) collective-permute-start(bf16[4,10,1,1024]{3,2,1,0:T(2,128)(2,1)S(1)} %get-tuple-element.73), channel_id=1, source_target_pairs={{1,0},{2,1},{3,2},{4,3},{5,4},{6,5},{7,6},{9,8},{10,9},{11,10},{12... | collective-permute-start | bytes 245768 | tf_op jit(solution)/shard_map/ppermute | solution.py:17
  374.2 25.5 %collective-permute-start.18 = (bf16[4,10,1,1024]{3,2,1,0:T(2,128)(2,1)S(1)}, bf16[4,10,1,1024]{3,2,1,0:T(2,128)(2,1)S(1)}, u32[]{:S(2)}, u32[]{:S(2)}) collective-permute-start(bf16[4,10,1,1024]{3,2,1,0:T(2,128)(2,1)S(1)} %get-tuple-element.72), channel_id=1, source_target_pairs={{0,1},{1,2},{2,3},{3,4},{4,5},{5,6},{6,7},{8,9},{9,10},{10,11},{11... | collective-permute-start | bytes 245768 | tf_op jit(solution)/shard_map/ppermute | solution.py:16
  377.3 50.0 %collective-permute-start.31 = (bf16[4,10,1,1024]{3,2,1,0:T(2,128)(2,1)S(1)}, bf16[4,10,1,1024]{3,2,1,0:T(2,128)(2,1)S(1)}, u32[]{:S(2)}, u32[]{:S(2)}) collective-permute-start(bf16[4,10,1,1024]{3,2,1,0:T(2,128)(2,1)S(1)} %get-tuple-element.71), channel_id=1, source_target_pairs={{1,0},{2,1},{3,2},{4,3},{5,4},{6,5},{7,6},{9,8},{10,9},{11,10},{12... | collective-permute-start | bytes 245768 | tf_op jit(solution)/shard_map/ppermute | solution.py:17
  380.5 8.6 %collective-permute-start.3 = (f32[4,10,1,1024]{3,2,1,0:T(1,128)S(1)}, f32[4,10,1,1024]{3,2,1,0:T(1,128)S(1)}, u32[]{:S(2)}, u32[]{:S(2)}) collective-permute-start(f32[4,10,1,1024]{3,2,1,0:T(1,128)S(1)} %get-tuple-element.47), channel_id=1, source_target_pairs={{0,1},{1,2},{2,3},{3,4},{4,5},{5,6},{6,7},{8,9},{9,10},{10,11},{11... | collective-permute-start | bytes 491528 | tf_op jit(solution)/shard_map/ppermute | solution.py:16
  384.1 8.7 %collective-permute-start.2 = (f32[4,10,1,1024]{3,2,1,0:T(1,128)S(1)}, f32[4,10,1,1024]{3,2,1,0:T(1,128)S(1)}, u32[]{:S(2)}, u32[]{:S(2)}) collective-permute-start(f32[4,10,1,1024]{3,2,1,0:T(1,128)S(1)} %get-tuple-element.46), channel_id=1, source_target_pairs={{1,0},{2,1},{3,2},{4,3},{5,4},{6,5},{7,6},{9,8},{10,9},{11,10},{12... | collective-permute-start | bytes 491528 | tf_op jit(solution)/shard_map/ppermute | solution.py:17
  389.0 7.7 %copy-start.1 = (f32[8,8,1024]{2,1,0:T(8,128)S(1)}, f32[8,8,1024]{2,1,0:T(8,128)}, u32[]{:S(2)}) copy-start(f32[8,8,1024]{2,1,0:T(8,128)} %param.8) | copy-start | bytes 786436
  389.0 7.7 %copy-start.4 = (f32[8,8,1024]{2,1,0:T(8,128)S(1)}, f32[8,8,1024]{2,1,0:T(8,128)}, u32[]{:S(2)}) copy-start(f32[8,8,1024]{2,1,0:T(8,128)} %reshape.127) | copy-start | bytes 786436
  389.1 40.2 %collective-permute-start.30 = (bf16[4,10,1,1024]{3,2,1,0:T(2,128)(2,1)S(1)}, bf16[4,10,1,1024]{3,2,1,0:T(2,128)(2,1)S(1)}, u32[]{:S(2)}, u32[]{:S(2)}) collective-permute-start(bf16[4,10,1,1024]{3,2,1,0:T(2,128)(2,1)S(1)} %get-tuple-element.70), channel_id=1, source_target_pairs={{0,1},{1,2},{2,3},{3,4},{4,5},{5,6},{6,7},{8,9},{9,10},{10,11},{11... | collective-permute-start | bytes 245768 | tf_op jit(solution)/shard_map/ppermute | solution.py:16
  392.9 54.9 %collective-permute-start.43 = (bf16[4,10,1,1024]{3,2,1,0:T(2,128)(2,1)S(1)}, bf16[4,10,1,1024]{3,2,1,0:T(2,128)(2,1)S(1)}, u32[]{:S(2)}, u32[]{:S(2)}) collective-permute-start(bf16[4,10,1,1024]{3,2,1,0:T(2,128)(2,1)S(1)} %get-tuple-element.69), channel_id=1, source_target_pairs={{1,0},{2,1},{3,2},{4,3},{5,4},{6,5},{7,6},{9,8},{10,9},{11,10},{12... | collective-permute-start | bytes 245768 | tf_op jit(solution)/shard_map/ppermute | solution.py:17
  397.1 5.4 collective-permute-start.9
  399.6 4.7 collective-permute-start.8
  404.4 7.6 %collective-permute-start.11 = (f32[10,1,1024]{2,1,0:T(1,128)S(1)}, f32[10,1,1024]{2,1,0:T(1,128)S(1)}, u32[]{:S(2)}, u32[]{:S(2)}) collective-permute-start(f32[10,1,1024]{2,1,0:T(1,128)S(1)} %get-tuple-element.99), channel_id=1, source_target_pairs={{0,1},{1,2},{2,3},{3,4},{4,5},{5,6},{6,7},{8,9},{9,10},{10,11},{11... | collective-permute-start | bytes 122888 | tf_op jit(solution)/shard_map/ppermute | solution.py:16
  409.4 5.3 collective-permute-start.10
  415.5 4.5 collective-permute-start.13
  418.0 5.7 %collective-permute-start.12 = (f32[4,1,8,1024]{3,2,1,0:T(8,128)S(1)}, f32[4,1,8,1024]{3,2,1,0:T(8,128)S(1)}, u32[]{:S(2)}, u32[]{:S(2)}) collective-permute-start(f32[4,1,8,1024]{3,2,1,0:T(8,128)S(1)} %get-tuple-element.62), channel_id=1, source_target_pairs={{8,0},{16,8},{24,16},{32,24},{40,32},{48,40},{56,48},{9,1},{17,9},... | collective-permute-start | bytes 393224 | tf_op jit(solution)/shard_map/ppermute | solution.py:17
  420.0 27.8 %collective-permute-start.42 = (bf16[4,10,1,1024]{3,2,1,0:T(2,128)(2,1)S(1)}, bf16[4,10,1,1024]{3,2,1,0:T(2,128)(2,1)S(1)}, u32[]{:S(2)}, u32[]{:S(2)}) collective-permute-start(bf16[4,10,1,1024]{3,2,1,0:T(2,128)(2,1)S(1)} %get-tuple-element.68), channel_id=1, source_target_pairs={{0,1},{1,2},{2,3},{3,4},{4,5},{5,6},{6,7},{8,9},{9,10},{10,11},{11... | collective-permute-start | bytes 245768 | tf_op jit(solution)/shard_map/ppermute | solution.py:16
  423.9 6.0 %collective-permute-start.15 = (f32[4,10,1,1024]{3,2,1,0:T(1,128)S(1)}, f32[4,10,1,1024]{3,2,1,0:T(1,128)S(1)}, u32[]{:S(2)}, u32[]{:S(2)}) collective-permute-start(f32[4,10,1,1024]{3,2,1,0:T(1,128)S(1)} %get-tuple-element.43), channel_id=1, source_target_pairs={{0,1},{1,2},{2,3},{3,4},{4,5},{5,6},{6,7},{8,9},{9,10},{10,11},{11... | collective-permute-start | bytes 491528 | tf_op jit(solution)/shard_map/ppermute | solution.py:16
  427.3 6.6 %collective-permute-start.14 = (f32[4,10,1,1024]{3,2,1,0:T(1,128)S(1)}, f32[4,10,1,1024]{3,2,1,0:T(1,128)S(1)}, u32[]{:S(2)}, u32[]{:S(2)}) collective-permute-start(f32[4,10,1,1024]{3,2,1,0:T(1,128)S(1)} %get-tuple-element.42), channel_id=1, source_target_pairs={{1,0},{2,1},{3,2},{4,3},{5,4},{6,5},{7,6},{9,8},{10,9},{11,10},{12... | collective-permute-start | bytes 491528 | tf_op jit(solution)/shard_map/ppermute | solution.py:17
  429.9 5.1 copy-start.3
  435.4 4.5 collective-permute-start.21
  437.9 4.7 collective-permute-start.20
  442.6 5.8 %collective-permute-start.23 = (f32[10,1,1024]{2,1,0:T(1,128)S(1)}, f32[10,1,1024]{2,1,0:T(1,128)S(1)}, u32[]{:S(2)}, u32[]{:S(2)}) collective-permute-start(f32[10,1,1024]{2,1,0:T(1,128)S(1)} %get-tuple-element.95), channel_id=1, source_target_pairs={{0,1},{1,2},{2,3},{3,4},{4,5},{5,6},{6,7},{8,9},{9,10},{10,11},{11... | collective-permute-start | bytes 122888 | tf_op jit(solution)/shard_map/ppermute | solution.py:16
  445.8 5.3 collective-permute-start.22
  451.9 4.5 collective-permute-start.25
  454.4 5.7 %collective-permute-start.24 = (f32[4,1,8,1024]{3,2,1,0:T(8,128)S(1)}, f32[4,1,8,1024]{3,2,1,0:T(8,128)S(1)}, u32[]{:S(2)}, u32[]{:S(2)}) collective-permute-start(f32[4,1,8,1024]{3,2,1,0:T(8,128)S(1)} %get-tuple-element.57), channel_id=1, source_target_pairs={{8,0},{16,8},{24,16},{32,24},{40,32},{48,40},{56,48},{9,1},{17,9},... | collective-permute-start | bytes 393224 | tf_op jit(solution)/shard_map/ppermute | solution.py:17
  460.3 6.7 %collective-permute-start.27 = (f32[4,10,1,1024]{3,2,1,0:T(1,128)S(1)}, f32[4,10,1,1024]{3,2,1,0:T(1,128)S(1)}, u32[]{:S(2)}, u32[]{:S(2)}) collective-permute-start(f32[4,10,1,1024]{3,2,1,0:T(1,128)S(1)} %get-tuple-element.39), channel_id=1, source_target_pairs={{0,1},{1,2},{2,3},{3,4},{4,5},{5,6},{6,7},{8,9},{9,10},{10,11},{11... | collective-permute-start | bytes 491528 | tf_op jit(solution)/shard_map/ppermute | solution.py:16
  463.7 6.6 %collective-permute-start.26 = (f32[4,10,1,1024]{3,2,1,0:T(1,128)S(1)}, f32[4,10,1,1024]{3,2,1,0:T(1,128)S(1)}, u32[]{:S(2)}, u32[]{:S(2)}) collective-permute-start(f32[4,10,1,1024]{3,2,1,0:T(1,128)S(1)} %get-tuple-element.38), channel_id=1, source_target_pairs={{1,0},{2,1},{3,2},{4,3},{5,4},{6,5},{7,6},{9,8},{10,9},{11,10},{12... | collective-permute-start | bytes 491528 | tf_op jit(solution)/shard_map/ppermute | solution.py:17
  467.0 4.4 copy-start.2
  471.8 4.2 collective-permute-start.33
  474.4 4.7 collective-permute-start.32
  479.1 5.3 collective-permute-start.35
  482.3 5.3 collective-permute-start.34
  488.3 4.5 collective-permute-start.37
  490.9 5.7 %collective-permute-start.36 = (f32[4,1,8,1024]{3,2,1,0:T(8,128)S(1)}, f32[4,1,8,1024]{3,2,1,0:T(8,128)S(1)}, u32[]{:S(2)}, u32[]{:S(2)}) collective-permute-start(f32[4,1,8,1024]{3,2,1,0:T(8,128)S(1)} %get-tuple-element.52), channel_id=1, source_target_pairs={{8,0},{16,8},{24,16},{32,24},{40,32},{48,40},{56,48},{9,1},{17,9},... | collective-permute-start | bytes 393224 | tf_op jit(solution)/shard_map/ppermute | solution.py:17
  496.8 6.6 %collective-permute-start.39 = (f32[4,10,1,1024]{3,2,1,0:T(1,128)S(1)}, f32[4,10,1,1024]{3,2,1,0:T(1,128)S(1)}, u32[]{:S(2)}, u32[]{:S(2)}) collective-permute-start(f32[4,10,1,1024]{3,2,1,0:T(1,128)S(1)} %get-tuple-element.35), channel_id=1, source_target_pairs={{0,1},{1,2},{2,3},{3,4},{4,5},{5,6},{6,7},{8,9},{9,10},{10,11},{11... | collective-permute-start | bytes 491528 | tf_op jit(solution)/shard_map/ppermute | solution.py:16
  501.1 6.6 %collective-permute-start.38 = (f32[4,10,1,1024]{3,2,1,0:T(1,128)S(1)}, f32[4,10,1,1024]{3,2,1,0:T(1,128)S(1)}, u32[]{:S(2)}, u32[]{:S(2)}) collective-permute-start(f32[4,10,1,1024]{3,2,1,0:T(1,128)S(1)} %get-tuple-element.34), channel_id=1, source_target_pairs={{1,0},{2,1},{3,2},{4,3},{5,4},{6,5},{7,6},{9,8},{10,9},{11,10},{12... | collective-permute-start | bytes 491528 | tf_op jit(solution)/shard_map/ppermute | solution.py:17
  509.2 3.9 collective-permute-start.45
  511.4 4.7 collective-permute-start.44
  516.1 5.3 collective-permute-start.47
  519.3 5.3 collective-permute-start.46
Sparse Core Ops, SparseCore 0:
  527.4 21.7 reduce-scatter.1
where the time goes:
time: 559 us; the launch traced here: 556 us
  blocking collectives  279 us (50%)
  starting transfers between devices  124 us (22%)
  waiting for transfers between devices  64.3 us (12%)
  other arithmetic  39.6 us (7%)
  local copies, waits for them, and re-layouts  33.9 us (6%)
  between operations  15.8 us (3%)
    psum x1, blocking collectives, shards(): samples = lax.psum(local_samples, ('gx', 'gy'))  279 us
    ppermute x24, starting transfers between devices, extended(): before = lax.ppermute(last, axis, up)  76.4 us
    ppermute x24, starting transfers between devices, extended(): after = lax.ppermute(initial, axis, down)  47.4 us
    ppermute x24, waiting for transfers between devices, extended(): after = lax.ppermute(initial, axis, down)  42.7 us
    reduce_scatter x1, waiting for transfers between devices, shards(): lax.psum_scatter(kernel_local, 'pair', scatter_dimension=3, tiled=True)  20.9 us
    slice x2, local copies, waits for them, and re-layouts, shards(): pressure_snaps = forward_field[:, 0].reshape(steps_total, -1)  14.9 us
  transfers between devices with their start and end apart: 49, of which 18 were waited for; matrix products, arithmetic and copies ran while one was open for 11% of the time, Pallas kernels for 0%

commit v1 on v0

--- a/solution.py
+++ b/solution.py
@@ -62,7 +62,7 @@
     local_samples = (
         jnp.take(pressure_snaps, src_flat, axis=1).astype(jnp.float32) * src_inside[None, :]
     )
-    samples = lax.psum(local_samples, ("gx", "gy"))
+    samples = lax.psum(lax.psum(local_samples, "gy"), "gx")
     state = adjoint_state[0]
     kernel_local = jnp.zeros((4, width_x, width_y, depth), jnp.float32)
     for step in range(steps_total):

time: 559 us -> 348 us (0.62)
  blocking collectives: 279 us -> 57.5 us
  starting transfers between devices: 124 us -> 134 us
    psum x1 -> x2, blocking collectives: 279 us -> 57.5 us  [shards(): samples = lax.psum(lax.psum(local_samples, 'gy'), 'gx')]
    ppermute x24, starting transfers between devices: 76.4 us -> 83.2 us  [extended(): before = lax.ppermute(last, axis, up)]
  transfers between devices with their start and end apart: 49 -> 49, of which waited for: 18 -> 18; matrix products, arithmetic and copies ran while one was open for 11% -> 18% of each run, Pallas kernels for 0% -> 0%
where the time goes in v1:
time: 348 us; the launch traced here: 344 us
  starting transfers between devices  134 us (39%)
  waiting for transfers between devices  63.1 us (18%)
  blocking collectives  57.5 us (17%)
  other arithmetic  39.7 us (11%)
  local copies, waits for them, and re-layouts  34 us (10%)
  between operations  15.8 us (5%)
    ppermute x24, starting transfers between devices, extended(): before = lax.ppermute(last, axis, up)  83.2 us
    psum x2, blocking collectives, shards(): samples = lax.psum(lax.psum(local_samples, 'gy'), 'gx')  57.5 us
    ppermute x24, starting transfers between devices, extended(): after = lax.ppermute(initial, axis, down)  51.2 us
    ppermute x24, waiting for transfers between devices, extended(): after = lax.ppermute(initial, axis, down)  43.3 us
    reduce_scatter x1, waiting for transfers between devices, shards(): lax.psum_scatter(kernel_local, 'pair', scatter_dimension=3, tiled=True)  19.1 us
    slice x2, local copies, waits for them, and re-layouts, shards(): pressure_snaps = forward_field[:, 0].reshape(steps_total, -1)  15 us
    scatter-add x4, other arithmetic, shards(): injected = jnp.zeros((width_x * width_y * depth,), jnp.float32).at[rcv_fl...  9.35 us
    gather x1, local copies, waits for them, and re-layouts, shards(): jnp.take(pressure_snaps, src_flat, axis=1).astype(jnp.float32)  8.65 us
  transfers between devices with their start and end apart: 49, of which 18 were waited for; matrix products, arithmetic and copies ran while one was open for 18% of the time, Pallas kernels for 0%

profile of v1, /device:TPU:1, one launch (start us, length us, event | category | flops | bytes accessed | tf_op | source)
XLA Modules:
  0.0 344.5 jit_solution(7690591108701648118)
XLA Ops:
  7.2 1.8 slice_bitcast_fusion
  11.0 5.2 %collective-permute-start.4 = (bf16[4,1,8,1024]{3,2,1,0:T(8,128)(2,1)}, bf16[4,1,8,1024]{3,2,1,0:T(8,128)(2,1)}, u32[]{:S(2)}, u32[]{:S(2)}) collective-permute-start(bf16[4,1,8,1024]{3,2,1,0:T(8,128)(2,1)} %get-tuple-element.82), channel_id=1, source_target_pairs={{0,8},{8,16},{16,24},{24,32},{32,40},{40,48},{48,56},{1,9},{9,17},... | collective-permute-start | bytes 196616 | tf_op jit(solution)/shard_map/ppermute | solution.py:16
  17.0 3.6 %collective-permute-start.1 = (f32[4,1,8,1024]{3,2,1,0:T(8,128)}, f32[4,1,8,1024]{3,2,1,0:T(8,128)S(1)}, u32[]{:S(2)}, u32[]{:S(2)}) collective-permute-start(f32[4,1,8,1024]{3,2,1,0:T(8,128)} %get-tuple-element.66), channel_id=1, source_target_pairs={{0,8},{8,16},{16,24},{24,32},{32,40},{40,48},{48,56},{1,9},{9,17},... | collective-permute-start | bytes 393224 | tf_op jit(solution)/shard_map/ppermute | solution.py:16
  23.9 1.9 slice.831
  26.9 13.2 %copy.11 = bf16[4,1,8,8,1024]{0,4,3,2,1:T(8,128)(2,1)} copy(bf16[4,1,8,8,1024]{4,3,2,1,0:T(8,128)(2,1)} %slice.831) | data formatting | bytes 1048576 | tf_op jit(solution)/shard_map/slice | solution.py:61
  40.1 8.7 %gather_fusion = bf16[256,4]{1,0:T(8,128)(2,1)S(1)} fusion(bf16[4,65536]{0,1:T(8,128)(2,1)} %bitcast.532, s32[1024]{0:T(1024)S(1)} %pad_clamp_fusion), kind=kCustom, calls=%fused_computation | custom fusion | bytes 5120 | tf_op jit(solution)/shard_map/jit(_take)/gather | solution.py:63
  48.9 25.2 %psum.14 = f32[4,256]{0,1:T(8,128)S(1)} all-reduce(f32[4,256]{0,1:T(8,128)S(1)} %multiply_bitcast_fusion), channel_id=1, replica_groups=mesh['pair'=2,'gx'=8,'gy'=8] {'gy'}, use_global_device_ids=true, to_apply=%region_0.1 | all-reduce | flops 1024 | bytes 8192 | tf_op jit(solution)/shard_map/psum | solution.py:65
  74.2 32.2 %psum.15 = f32[4,256]{0,1:T(8,128)S(1)} all-reduce(f32[4,256]{0,1:T(8,128)S(1)} %psum.14), channel_id=1, replica_groups=mesh['pair'=2,'gx'=8,'gy'=8] {'gx'}, use_global_device_ids=true, to_apply=%region_1.2 | all-reduce | flops 1024 | bytes 8192 | tf_op jit(solution)/shard_map/psum | solution.py:65
  109.6 1.3 select_select_fusion
  111.5 2.2 scatter_custom_fusion
  114.4 2.2 scatter_custom_fusion.1
  117.3 2.2 scatter_custom_fusion.2
  120.3 2.8 scatter_custom_fusion.3
  127.9 4.0 %collective-permute-start.28 = (bf16[4,1,8,1024]{3,2,1,0:T(8,128)(2,1)}, bf16[4,1,8,1024]{3,2,1,0:T(8,128)(2,1)S(1)}, u32[]{:S(2)}, u32[]{:S(2)}) collective-permute-start(bf16[4,1,8,1024]{3,2,1,0:T(8,128)(2,1)} %get-tuple-element.78), channel_id=1, source_target_pairs={{0,8},{8,16},{16,24},{24,32},{32,40},{40,48},{48,56},{1,9},{9,17},... | collective-permute-start | bytes 196616 | tf_op jit(solution)/shard_map/ppermute | solution.py:16
  134.3 4.3 %collective-permute-start.40 = (bf16[4,1,8,1024]{3,2,1,0:T(8,128)(2,1)}, bf16[4,1,8,1024]{3,2,1,0:T(8,128)(2,1)S(1)}, u32[]{:S(2)}, u32[]{:S(2)}) collective-permute-start(bf16[4,1,8,1024]{3,2,1,0:T(8,128)(2,1)} %get-tuple-element.76), channel_id=1, source_target_pairs={{0,8},{8,16},{16,24},{24,32},{32,40},{40,48},{48,56},{1,9},{9,17},... | collective-permute-start | bytes 196616 | tf_op jit(solution)/shard_map/ppermute | solution.py:16
  138.7 13.7 %collective-permute-start.7 = (bf16[4,10,1,1024]{3,2,1,0:T(2,128)(2,1)S(1)}, bf16[4,10,1,1024]{3,2,1,0:T(2,128)(2,1)S(1)}, u32[]{:S(2)}, u32[]{:S(2)}) collective-permute-start(bf16[4,10,1,1024]{3,2,1,0:T(2,128)(2,1)S(1)} %get-tuple-element.75), channel_id=1, source_target_pairs={{1,0},{2,1},{3,2},{4,3},{5,4},{6,5},{7,6},{9,8},{10,9},{11,10},{12... | collective-permute-start | bytes 245768 | tf_op jit(solution)/shard_map/ppermute | solution.py:17
  152.6 1.9 collective-permute-start.6
  154.6 2.4 collective-permute-start.19
  157.2 3.2 collective-permute-start.18
  160.4 1.9 collective-permute-start.31
  163.5 3.6 %collective-permute-start.3 = (f32[4,10,1,1024]{3,2,1,0:T(1,128)S(1)}, f32[4,10,1,1024]{3,2,1,0:T(1,128)S(1)}, u32[]{:S(2)}, u32[]{:S(2)}) collective-permute-start(f32[4,10,1,1024]{3,2,1,0:T(1,128)S(1)} %get-tuple-element.47), channel_id=1, source_target_pairs={{0,1},{1,2},{2,3},{3,4},{4,5},{5,6},{6,7},{8,9},{9,10},{10,11},{11... | collective-permute-start | bytes 491528 | tf_op jit(solution)/shard_map/ppermute | solution.py:16
  167.2 2.1 collective-permute-start.2
  169.3 1.6 maximum_convert_fusion
  172.1 3.8 %collective-permute-start.30 = (bf16[4,10,1,1024]{3,2,1,0:T(2,128)(2,1)S(1)}, bf16[4,10,1,1024]{3,2,1,0:T(2,128)(2,1)S(1)}, u32[]{:S(2)}, u32[]{:S(2)}) collective-permute-start(bf16[4,10,1,1024]{3,2,1,0:T(2,128)(2,1)S(1)} %get-tuple-element.70), channel_id=1, source_target_pairs={{0,1},{1,2},{2,3},{3,4},{4,5},{5,6},{6,7},{8,9},{9,10},{10,11},{11... | collective-permute-start | bytes 245768 | tf_op jit(solution)/shard_map/ppermute | solution.py:16
  175.9 1.9 collective-permute-start.43
  177.8 1.9 fusion.39
  180.1 4.3 %collective-permute-start.9 = (f32[1,8,1024]{2,1,0:T(8,128)S(1)}, f32[1,8,1024]{2,1,0:T(8,128)S(1)}, u32[]{:S(2)}, u32[]{:S(2)}) collective-permute-start(f32[1,8,1024]{2,1,0:T(8,128)S(1)} %get-tuple-element.110), channel_id=1, source_target_pairs={{0,8},{8,16},{16,24},{24,32},{32,40},{40,48},{48,56},{1,9},{9,17},... | collective-permute-start | bytes 98312 | tf_op jit(solution)/shard_map/ppermute | solution.py:16
  185.8 1.5 maximum_convert_fusion.1
  187.3 1.8 collective-permute-done.8
  189.2 5.1 %collective-permute-start.11 = (f32[10,1,1024]{2,1,0:T(1,128)S(1)}, f32[10,1,1024]{2,1,0:T(1,128)S(1)}, u32[]{:S(2)}, u32[]{:S(2)}) collective-permute-start(f32[10,1,1024]{2,1,0:T(1,128)S(1)} %get-tuple-element.99), channel_id=1, source_target_pairs={{0,1},{1,2},{2,3},{3,4},{4,5},{5,6},{6,7},{8,9},{9,10},{10,11},{11... | collective-permute-start | bytes 122888 | tf_op jit(solution)/shard_map/ppermute | solution.py:16
  194.3 1.9 collective-permute-start.10
  196.8 2.8 collective-permute-done.10
  200.3 2.5 collective-permute-start.13
  204.8 2.7 collective-permute-start.42
  208.8 3.3 collective-permute-start.15
  212.1 1.9 collective-permute-start.14
  214.8 4.0 %collective-permute-done.14 = f32[4,10,1,1024]{3,2,1,0:T(1,128)S(1)} collective-permute-done((f32[4,10,1,1024]{3,2,1,0:T(1,128)S(1)}, f32[4,10,1,1024]{3,2,1,0:T(1,128)S(1)}, u32[]{:S(2)}, u32[]{:S(2)}) %collective-permute-start.14) | collective-permute-done | bytes 163872 | tf_op jit(solution)/shard_map/ppermute | solution.py:17
  220.2 3.6 %collective-permute-start.21 = (f32[1,8,1024]{2,1,0:T(8,128)S(1)}, f32[1,8,1024]{2,1,0:T(8,128)S(1)}, u32[]{:S(2)}, u32[]{:S(2)}) collective-permute-start(f32[1,8,1024]{2,1,0:T(8,128)S(1)} %get-tuple-element.107), channel_id=1, source_target_pairs={{0,8},{8,16},{16,24},{24,32},{32,40},{40,48},{48,56},{1,9},{9,17},... | collective-permute-start | bytes 98312 | tf_op jit(solution)/shard_map/ppermute | solution.py:16
  225.7 2.8 collective-permute-done.20
  228.5 3.1 collective-permute-start.23
  231.7 1.9 collective-permute-start.22
  234.3 2.7 collective-permute-done.22
  237.7 4.3 %collective-permute-start.25 = (f32[4,1,8,1024]{3,2,1,0:T(8,128)S(1)}, f32[4,1,8,1024]{3,2,1,0:T(8,128)S(1)}, u32[]{:S(2)}, u32[]{:S(2)}) collective-permute-start(f32[4,1,8,1024]{3,2,1,0:T(8,128)S(1)} %get-tuple-element.56), channel_id=1, source_target_pairs={{0,8},{8,16},{16,24},{24,32},{32,40},{40,48},{48,56},{1,9},{9,17},... | collective-permute-start | bytes 393224 | tf_op jit(solution)/shard_map/ppermute | solution.py:16
  243.9 4.3 %collective-permute-done.24 = f32[4,1,8,1024]{3,2,1,0:T(8,128)S(1)} collective-permute-done((f32[4,1,8,1024]{3,2,1,0:T(8,128)S(1)}, f32[4,1,8,1024]{3,2,1,0:T(8,128)S(1)}, u32[]{:S(2)}, u32[]{:S(2)}) %collective-permute-start.24) | collective-permute-done | bytes 131104 | tf_op jit(solution)/shard_map/ppermute | solution.py:17
  248.5 3.1 collective-permute-start.27
  251.5 2.1 collective-permute-start.26
  254.9 3.2 collective-permute-done.26
  259.6 3.9 %collective-permute-start.33 = (f32[1,8,1024]{2,1,0:T(8,128)S(1)}, f32[1,8,1024]{2,1,0:T(8,128)S(1)}, u32[]{:S(2)}, u32[]{:S(2)}) collective-permute-start(f32[1,8,1024]{2,1,0:T(8,128)S(1)} %get-tuple-element.104), channel_id=1, source_target_pairs={{0,8},{8,16},{16,24},{24,32},{32,40},{40,48},{48,56},{1,9},{9,17},... | collective-permute-start | bytes 98312 | tf_op jit(solution)/shard_map/ppermute | solution.py:16
  265.2 3.0 collective-permute-done.32
  268.3 3.2 collective-permute-start.35
  271.5 1.9 collective-permute-start.34
  273.6 3.2 collective-permute-done.34
  277.5 3.5 %collective-permute-start.37 = (f32[4,1,8,1024]{3,2,1,0:T(8,128)S(1)}, f32[4,1,8,1024]{3,2,1,0:T(8,128)S(1)}, u32[]{:S(2)}, u32[]{:S(2)}) collective-permute-start(f32[4,1,8,1024]{3,2,1,0:T(8,128)S(1)} %get-tuple-element.51), channel_id=1, source_target_pairs={{0,8},{8,16},{16,24},{24,32},{32,40},{40,48},{48,56},{1,9},{9,17},... | collective-permute-start | bytes 393224 | tf_op jit(solution)/shard_map/ppermute | solution.py:16
  282.9 3.8 %collective-permute-done.36 = f32[4,1,8,1024]{3,2,1,0:T(8,128)S(1)} collective-permute-done((f32[4,1,8,1024]{3,2,1,0:T(8,128)S(1)}, f32[4,1,8,1024]{3,2,1,0:T(8,128)S(1)}, u32[]{:S(2)}, u32[]{:S(2)}) %collective-permute-start.36) | collective-permute-done | bytes 131104 | tf_op jit(solution)/shard_map/ppermute | solution.py:17
  286.9 3.8 %collective-permute-start.39 = (f32[4,10,1,1024]{3,2,1,0:T(1,128)S(1)}, f32[4,10,1,1024]{3,2,1,0:T(1,128)S(1)}, u32[]{:S(2)}, u32[]{:S(2)}) collective-permute-start(f32[4,10,1,1024]{3,2,1,0:T(1,128)S(1)} %get-tuple-element.35), channel_id=1, source_target_pairs={{0,1},{1,2},{2,3},{3,4},{4,5},{5,6},{6,7},{8,9},{9,10},{10,11},{11... | collective-permute-start | bytes 491528 | tf_op jit(solution)/shard_map/ppermute | solution.py:16
  290.7 1.9 collective-permute-start.38
  292.9 4.4 %collective-permute-done.38 = f32[4,10,1,1024]{3,2,1,0:T(1,128)S(1)} collective-permute-done((f32[4,10,1,1024]{3,2,1,0:T(1,128)S(1)}, f32[4,10,1,1024]{3,2,1,0:T(1,128)S(1)}, u32[]{:S(2)}, u32[]{:S(2)}) %collective-permute-start.38) | collective-permute-done | bytes 163872 | tf_op jit(solution)/shard_map/ppermute | solution.py:17
  298.8 2.8 collective-permute-start.45
  303.3 3.0 collective-permute-done.44
  306.3 3.2 collective-permute-start.47
  309.5 1.9 collective-permute-start.46
  311.6 3.2 collective-permute-done.46
  316.0 1.5 fusion.41
  318.6 19.1 %reduce-scatter.2.cloned.1.call-done = f32[4,8,8,512]{3,2,1,0:T(8,128)} async-done(((f32[4,8,8,1024]{3,2,1,0:T(8,128)}), f32[4,8,8,512]{3,2,1,0:T(8,128)}) %reduce-scatter.2.cloned.1.call-update) | async-done | bytes 524304 | tf_op jit(solution)/shard_map/reduce_scatter | solution.py:112
  (139 shorter events, 49.6 us)
Async XLA Ops:
  7.2 9.1 %copy-start = (f32[1,4,8,8,1024]{4,3,2,1,0:T(8,128)S(1)}, f32[1,4,8,8,1024]{4,3,2,1,0:T(8,128)}, u32[]{:S(2)}) copy-start(f32[1,4,8,8,1024]{4,3,2,1,0:T(8,128)} %param.11) | copy-start | bytes 3145732
  7.2 18.6 %copy-start.6 = (f32[256,4]{0,1:T(4,128)S(1)}, f32[256,4]{0,1:T(4,128)}, u32[]{:S(2)}) copy-start(f32[256,4]{0,1:T(4,128)} %param.15) | copy-start | bytes 12292
  7.2 19.2 %copy-start.5 = (s32[256,3]{0,1:T(4,128)S(1)}, s32[256,3]{0,1:T(4,128)}, u32[]{:S(2)}) copy-start(s32[256,3]{0,1:T(4,128)} %param.14) | copy-start | bytes 9220
  7.2 19.7 %copy-start.7 = (s32[256,3]{0,1:T(4,128)S(1)}, s32[256,3]{0,1:T(4,128)}, u32[]{:S(2)}) copy-start(s32[256,3]{0,1:T(4,128)} %param.13) | copy-start | bytes 9220
  7.2 330.4 %reduce-scatter.2.cloned.1.call-start = ((), (), s32[]{:S(2)}) async-start(), calls=%async_computation.1 | async-start | bytes 1572864 | tf_op jit(solution)/shard_map/reduce_scatter | solution.py:112
  9.8 114.3 %collective-permute-start.5 = (bf16[4,1,8,1024]{3,2,1,0:T(8,128)(2,1)}, bf16[4,1,8,1024]{3,2,1,0:T(8,128)(2,1)}, u32[]{:S(2)}, u32[]{:S(2)}) collective-permute-start(bf16[4,1,8,1024]{3,2,1,0:T(8,128)(2,1)} %get-tuple-element.83), channel_id=1, source_target_pairs={{8,0},{16,8},{24,16},{32,24},{40,32},{48,40},{56,48},{9,1},{17,9},... | collective-permute-start | bytes 196616 | tf_op jit(solution)/shard_map/ppermute | solution.py:17
  11.0 114.4 %collective-permute-start.4 = (bf16[4,1,8,1024]{3,2,1,0:T(8,128)(2,1)}, bf16[4,1,8,1024]{3,2,1,0:T(8,128)(2,1)}, u32[]{:S(2)}, u32[]{:S(2)}) collective-permute-start(bf16[4,1,8,1024]{3,2,1,0:T(8,128)(2,1)} %get-tuple-element.82), channel_id=1, source_target_pairs={{0,8},{8,16},{16,24},{24,32},{32,40},{40,48},{48,56},{1,9},{9,17},... | collective-permute-start | bytes 196616 | tf_op jit(solution)/shard_map/ppermute | solution.py:16
  17.0 140.2 %collective-permute-start.1 = (f32[4,1,8,1024]{3,2,1,0:T(8,128)}, f32[4,1,8,1024]{3,2,1,0:T(8,128)S(1)}, u32[]{:S(2)}, u32[]{:S(2)}) collective-permute-start(f32[4,1,8,1024]{3,2,1,0:T(8,128)} %get-tuple-element.66), channel_id=1, source_target_pairs={{0,8},{8,16},{16,24},{24,32},{32,40},{40,48},{48,56},{1,9},{9,17},... | collective-permute-start | bytes 393224 | tf_op jit(solution)/shard_map/ppermute | solution.py:16
  20.6 139.7 %collective-permute-start = (f32[4,1,8,1024]{3,2,1,0:T(8,128)}, f32[4,1,8,1024]{3,2,1,0:T(8,128)}, u32[]{:S(2)}, u32[]{:S(2)}) collective-permute-start(f32[4,1,8,1024]{3,2,1,0:T(8,128)} %get-tuple-element.67), channel_id=1, source_target_pairs={{8,0},{16,8},{24,16},{32,24},{40,32},{48,40},{56,48},{9,1},{17,9},... | collective-permute-start | bytes 393224 | tf_op jit(solution)/shard_map/ppermute | solution.py:17
  22.6 105.3 %collective-permute-start.17 = (bf16[4,1,8,1024]{3,2,1,0:T(8,128)(2,1)}, bf16[4,1,8,1024]{3,2,1,0:T(8,128)(2,1)}, u32[]{:S(2)}, u32[]{:S(2)}) collective-permute-start(bf16[4,1,8,1024]{3,2,1,0:T(8,128)(2,1)} %get-tuple-element.81), channel_id=1, source_target_pairs={{8,0},{16,8},{24,16},{32,24},{40,32},{48,40},{56,48},{9,1},{17,9},... | collective-permute-start | bytes 196616 | tf_op jit(solution)/shard_map/ppermute | solution.py:17
  124.1 7.8 %collective-permute-start.16 = (bf16[4,1,8,1024]{3,2,1,0:T(8,128)(2,1)}, bf16[4,1,8,1024]{3,2,1,0:T(8,128)(2,1)S(1)}, u32[]{:S(2)}, u32[]{:S(2)}) collective-permute-start(bf16[4,1,8,1024]{3,2,1,0:T(8,128)(2,1)} %get-tuple-element.80), channel_id=1, source_target_pairs={{0,8},{8,16},{16,24},{24,32},{32,40},{40,48},{48,56},{1,9},{9,17},... | collective-permute-start | bytes 196616 | tf_op jit(solution)/shard_map/ppermute | solution.py:16
  125.4 8.9 %collective-permute-start.29 = (bf16[4,1,8,1024]{3,2,1,0:T(8,128)(2,1)}, bf16[4,1,8,1024]{3,2,1,0:T(8,128)(2,1)S(1)}, u32[]{:S(2)}, u32[]{:S(2)}) collective-permute-start(bf16[4,1,8,1024]{3,2,1,0:T(8,128)(2,1)} %get-tuple-element.79), channel_id=1, source_target_pairs={{8,0},{16,8},{24,16},{32,24},{40,32},{48,40},{56,48},{9,1},{17,9},... | collective-permute-start | bytes 196616 | tf_op jit(solution)/shard_map/ppermute | solution.py:17
  127.9 10.8 %collective-permute-start.28 = (bf16[4,1,8,1024]{3,2,1,0:T(8,128)(2,1)}, bf16[4,1,8,1024]{3,2,1,0:T(8,128)(2,1)S(1)}, u32[]{:S(2)}, u32[]{:S(2)}) collective-permute-start(bf16[4,1,8,1024]{3,2,1,0:T(8,128)(2,1)} %get-tuple-element.78), channel_id=1, source_target_pairs={{0,8},{8,16},{16,24},{24,32},{32,40},{40,48},{48,56},{1,9},{9,17},... | collective-permute-start | bytes 196616 | tf_op jit(solution)/shard_map/ppermute | solution.py:16
  131.9 20.7 %collective-permute-start.41 = (bf16[4,1,8,1024]{3,2,1,0:T(8,128)(2,1)}, bf16[4,1,8,1024]{3,2,1,0:T(8,128)(2,1)S(1)}, u32[]{:S(2)}, u32[]{:S(2)}) collective-permute-start(bf16[4,1,8,1024]{3,2,1,0:T(8,128)(2,1)} %get-tuple-element.77), channel_id=1, source_target_pairs={{8,0},{16,8},{24,16},{32,24},{40,32},{48,40},{56,48},{9,1},{17,9},... | collective-permute-start | bytes 196616 | tf_op jit(solution)/shard_map/ppermute | solution.py:17
  134.3 20.2 %collective-permute-start.40 = (bf16[4,1,8,1024]{3,2,1,0:T(8,128)(2,1)}, bf16[4,1,8,1024]{3,2,1,0:T(8,128)(2,1)S(1)}, u32[]{:S(2)}, u32[]{:S(2)}) collective-permute-start(bf16[4,1,8,1024]{3,2,1,0:T(8,128)(2,1)} %get-tuple-element.76), channel_id=1, source_target_pairs={{0,8},{8,16},{16,24},{24,32},{32,40},{40,48},{48,56},{1,9},{9,17},... | collective-permute-start | bytes 196616 | tf_op jit(solution)/shard_map/ppermute | solution.py:16
  138.7 24.8 %collective-permute-start.7 = (bf16[4,10,1,1024]{3,2,1,0:T(2,128)(2,1)S(1)}, bf16[4,10,1,1024]{3,2,1,0:T(2,128)(2,1)S(1)}, u32[]{:S(2)}, u32[]{:S(2)}) collective-permute-start(bf16[4,10,1,1024]{3,2,1,0:T(2,128)(2,1)S(1)} %get-tuple-element.75), channel_id=1, source_target_pairs={{1,0},{2,1},{3,2},{4,3},{5,4},{6,5},{7,6},{9,8},{10,9},{11,10},{12... | collective-permute-start | bytes 245768 | tf_op jit(solution)/shard_map/ppermute | solution.py:17
  152.6 14.5 %collective-permute-start.6 = (bf16[4,10,1,1024]{3,2,1,0:T(2,128)(2,1)S(1)}, bf16[4,10,1,1024]{3,2,1,0:T(2,128)(2,1)S(1)}, u32[]{:S(2)}, u32[]{:S(2)}) collective-permute-start(bf16[4,10,1,1024]{3,2,1,0:T(2,128)(2,1)S(1)} %get-tuple-element.74), channel_id=1, source_target_pairs={{0,1},{1,2},{2,3},{3,4},{4,5},{5,6},{6,7},{8,9},{9,10},{10,11},{11... | collective-permute-start | bytes 245768 | tf_op jit(solution)/shard_map/ppermute | solution.py:16
  154.6 25.6 %collective-permute-start.19 = (bf16[4,10,1,1024]{3,2,1,0:T(2,128)(2,1)S(1)}, bf16[4,10,1,1024]{3,2,1,0:T(2,128)(2,1)S(1)}, u32[]{:S(2)}, u32[]{:S(2)}) collective-permute-start(bf16[4,10,1,1024]{3,2,1,0:T(2,128)(2,1)S(1)} %get-tuple-element.73), channel_id=1, source_target_pairs={{1,0},{2,1},{3,2},{4,3},{5,4},{6,5},{7,6},{9,8},{10,9},{11,10},{12... | collective-permute-start | bytes 245768 | tf_op jit(solution)/shard_map/ppermute | solution.py:17
  157.2 27.2 %collective-permute-start.18 = (bf16[4,10,1,1024]{3,2,1,0:T(2,128)(2,1)S(1)}, bf16[4,10,1,1024]{3,2,1,0:T(2,128)(2,1)S(1)}, u32[]{:S(2)}, u32[]{:S(2)}) collective-permute-start(bf16[4,10,1,1024]{3,2,1,0:T(2,128)(2,1)S(1)} %get-tuple-element.72), channel_id=1, source_target_pairs={{0,1},{1,2},{2,3},{3,4},{4,5},{5,6},{6,7},{8,9},{9,10},{10,11},{11... | collective-permute-start | bytes 245768 | tf_op jit(solution)/shard_map/ppermute | solution.py:16
  160.4 51.7 %collective-permute-start.31 = (bf16[4,10,1,1024]{3,2,1,0:T(2,128)(2,1)S(1)}, bf16[4,10,1,1024]{3,2,1,0:T(2,128)(2,1)S(1)}, u32[]{:S(2)}, u32[]{:S(2)}) collective-permute-start(bf16[4,10,1,1024]{3,2,1,0:T(2,128)(2,1)S(1)} %get-tuple-element.71), channel_id=1, source_target_pairs={{1,0},{2,1},{3,2},{4,3},{5,4},{6,5},{7,6},{9,8},{10,9},{11,10},{12... | collective-permute-start | bytes 245768 | tf_op jit(solution)/shard_map/ppermute | solution.py:17
  163.5 8.6 %collective-permute-start.3 = (f32[4,10,1,1024]{3,2,1,0:T(1,128)S(1)}, f32[4,10,1,1024]{3,2,1,0:T(1,128)S(1)}, u32[]{:S(2)}, u32[]{:S(2)}) collective-permute-start(f32[4,10,1,1024]{3,2,1,0:T(1,128)S(1)} %get-tuple-element.47), channel_id=1, source_target_pairs={{0,1},{1,2},{2,3},{3,4},{4,5},{5,6},{6,7},{8,9},{9,10},{10,11},{11... | collective-permute-start | bytes 491528 | tf_op jit(solution)/shard_map/ppermute | solution.py:16
  167.2 8.7 %collective-permute-start.2 = (f32[4,10,1,1024]{3,2,1,0:T(1,128)S(1)}, f32[4,10,1,1024]{3,2,1,0:T(1,128)S(1)}, u32[]{:S(2)}, u32[]{:S(2)}) collective-permute-start(f32[4,10,1,1024]{3,2,1,0:T(1,128)S(1)} %get-tuple-element.46), channel_id=1, source_target_pairs={{1,0},{2,1},{3,2},{4,3},{5,4},{6,5},{7,6},{9,8},{10,9},{11,10},{12... | collective-permute-start | bytes 491528 | tf_op jit(solution)/shard_map/ppermute | solution.py:17
  172.1 7.7 %copy-start.1 = (f32[8,8,1024]{2,1,0:T(8,128)S(1)}, f32[8,8,1024]{2,1,0:T(8,128)}, u32[]{:S(2)}) copy-start(f32[8,8,1024]{2,1,0:T(8,128)} %param.8) | copy-start | bytes 786436
  172.1 7.7 %copy-start.4 = (f32[8,8,1024]{2,1,0:T(8,128)S(1)}, f32[8,8,1024]{2,1,0:T(8,128)}, u32[]{:S(2)}) copy-start(f32[8,8,1024]{2,1,0:T(8,128)} %reshape.127) | copy-start | bytes 786436
  172.1 41.9 %collective-permute-start.30 = (bf16[4,10,1,1024]{3,2,1,0:T(2,128)(2,1)S(1)}, bf16[4,10,1,1024]{3,2,1,0:T(2,128)(2,1)S(1)}, u32[]{:S(2)}, u32[]{:S(2)}) collective-permute-start(bf16[4,10,1,1024]{3,2,1,0:T(2,128)(2,1)S(1)} %get-tuple-element.70), channel_id=1, source_target_pairs={{0,1},{1,2},{2,3},{3,4},{4,5},{5,6},{6,7},{8,9},{9,10},{10,11},{11... | collective-permute-start | bytes 245768 | tf_op jit(solution)/shard_map/ppermute | solution.py:16
  175.9 57.7 %collective-permute-start.43 = (bf16[4,10,1,1024]{3,2,1,0:T(2,128)(2,1)S(1)}, bf16[4,10,1,1024]{3,2,1,0:T(2,128)(2,1)S(1)}, u32[]{:S(2)}, u32[]{:S(2)}) collective-permute-start(bf16[4,10,1,1024]{3,2,1,0:T(2,128)(2,1)S(1)} %get-tuple-element.69), channel_id=1, source_target_pairs={{1,0},{2,1},{3,2},{4,3},{5,4},{6,5},{7,6},{9,8},{10,9},{11,10},{12... | collective-permute-start | bytes 245768 | tf_op jit(solution)/shard_map/ppermute | solution.py:17
  180.1 7.1 %collective-permute-start.9 = (f32[1,8,1024]{2,1,0:T(8,128)S(1)}, f32[1,8,1024]{2,1,0:T(8,128)S(1)}, u32[]{:S(2)}, u32[]{:S(2)}) collective-permute-start(f32[1,8,1024]{2,1,0:T(8,128)S(1)} %get-tuple-element.110), channel_id=1, source_target_pairs={{0,8},{8,16},{16,24},{24,32},{32,40},{40,48},{48,56},{1,9},{9,17},... | collective-permute-start | bytes 98312 | tf_op jit(solution)/shard_map/ppermute | solution.py:16
  184.5 4.7 %collective-permute-start.8 = (f32[1,8,1024]{2,1,0:T(8,128)S(1)}, f32[1,8,1024]{2,1,0:T(8,128)S(1)}, u32[]{:S(2)}, u32[]{:S(2)}) collective-permute-start(f32[1,8,1024]{2,1,0:T(8,128)S(1)} %get-tuple-element.111), channel_id=1, source_target_pairs={{8,0},{16,8},{24,16},{32,24},{40,32},{48,40},{56,48},{9,1},{17,9},... | collective-permute-start | bytes 98312 | tf_op jit(solution)/shard_map/ppermute | solution.py:17
  189.2 7.6 %collective-permute-start.11 = (f32[10,1,1024]{2,1,0:T(1,128)S(1)}, f32[10,1,1024]{2,1,0:T(1,128)S(1)}, u32[]{:S(2)}, u32[]{:S(2)}) collective-permute-start(f32[10,1,1024]{2,1,0:T(1,128)S(1)} %get-tuple-element.99), channel_id=1, source_target_pairs={{0,1},{1,2},{2,3},{3,4},{4,5},{5,6},{6,7},{8,9},{9,10},{10,11},{11... | collective-permute-start | bytes 122888 | tf_op jit(solution)/shard_map/ppermute | solution.py:16
  194.3 5.3 %collective-permute-start.10 = (f32[10,1,1024]{2,1,0:T(1,128)S(1)}, f32[10,1,1024]{2,1,0:T(1,128)S(1)}, u32[]{:S(2)}, u32[]{:S(2)}) collective-permute-start(f32[10,1,1024]{2,1,0:T(1,128)S(1)} %get-tuple-element.98), channel_id=1, source_target_pairs={{1,0},{2,1},{3,2},{4,3},{5,4},{6,5},{7,6},{9,8},{10,9},{11,10},{12... | collective-permute-start | bytes 122888 | tf_op jit(solution)/shard_map/ppermute | solution.py:17
  200.3 4.5 %collective-permute-start.13 = (f32[4,1,8,1024]{3,2,1,0:T(8,128)S(1)}, f32[4,1,8,1024]{3,2,1,0:T(8,128)S(1)}, u32[]{:S(2)}, u32[]{:S(2)}) collective-permute-start(f32[4,1,8,1024]{3,2,1,0:T(8,128)S(1)} %get-tuple-element.61), channel_id=1, source_target_pairs={{0,8},{8,16},{16,24},{24,32},{32,40},{40,48},{48,56},{1,9},{9,17},... | collective-permute-start | bytes 393224 | tf_op jit(solution)/shard_map/ppermute | solution.py:16
  202.9 5.8 %collective-permute-start.12 = (f32[4,1,8,1024]{3,2,1,0:T(8,128)S(1)}, f32[4,1,8,1024]{3,2,1,0:T(8,128)S(1)}, u32[]{:S(2)}, u32[]{:S(2)}) collective-permute-start(f32[4,1,8,1024]{3,2,1,0:T(8,128)S(1)} %get-tuple-element.62), channel_id=1, source_target_pairs={{8,0},{16,8},{24,16},{32,24},{40,32},{48,40},{56,48},{9,1},{17,9},... | collective-permute-start | bytes 393224 | tf_op jit(solution)/shard_map/ppermute | solution.py:17
  204.8 28.8 %collective-permute-start.42 = (bf16[4,10,1,1024]{3,2,1,0:T(2,128)(2,1)S(1)}, bf16[4,10,1,1024]{3,2,1,0:T(2,128)(2,1)S(1)}, u32[]{:S(2)}, u32[]{:S(2)}) collective-permute-start(bf16[4,10,1,1024]{3,2,1,0:T(2,128)(2,1)S(1)} %get-tuple-element.68), channel_id=1, source_target_pairs={{0,1},{1,2},{2,3},{3,4},{4,5},{5,6},{6,7},{8,9},{9,10},{10,11},{11... | collective-permute-start | bytes 245768 | tf_op jit(solution)/shard_map/ppermute | solution.py:16
  208.8 5.9 %collective-permute-start.15 = (f32[4,10,1,1024]{3,2,1,0:T(1,128)S(1)}, f32[4,10,1,1024]{3,2,1,0:T(1,128)S(1)}, u32[]{:S(2)}, u32[]{:S(2)}) collective-permute-start(f32[4,10,1,1024]{3,2,1,0:T(1,128)S(1)} %get-tuple-element.43), channel_id=1, source_target_pairs={{0,1},{1,2},{2,3},{3,4},{4,5},{5,6},{6,7},{8,9},{9,10},{10,11},{11... | collective-permute-start | bytes 491528 | tf_op jit(solution)/shard_map/ppermute | solution.py:16
  212.1 6.6 %collective-permute-start.14 = (f32[4,10,1,1024]{3,2,1,0:T(1,128)S(1)}, f32[4,10,1,1024]{3,2,1,0:T(1,128)S(1)}, u32[]{:S(2)}, u32[]{:S(2)}) collective-permute-start(f32[4,10,1,1024]{3,2,1,0:T(1,128)S(1)} %get-tuple-element.42), channel_id=1, source_target_pairs={{1,0},{2,1},{3,2},{4,3},{5,4},{6,5},{7,6},{9,8},{10,9},{11,10},{12... | collective-permute-start | bytes 491528 | tf_op jit(solution)/shard_map/ppermute | solution.py:17
  214.7 5.1 %copy-start.3 = (f32[8,8,1024]{2,1,0:T(8,128)S(1)}, f32[8,8,1024]{2,1,0:T(8,128)}, u32[]{:S(2)}) copy-start(f32[8,8,1024]{2,1,0:T(8,128)} %reshape.128) | copy-start | bytes 786436
  220.2 5.5 %collective-permute-start.21 = (f32[1,8,1024]{2,1,0:T(8,128)S(1)}, f32[1,8,1024]{2,1,0:T(8,128)S(1)}, u32[]{:S(2)}, u32[]{:S(2)}) collective-permute-start(f32[1,8,1024]{2,1,0:T(8,128)S(1)} %get-tuple-element.107), channel_id=1, source_target_pairs={{0,8},{8,16},{16,24},{24,32},{32,40},{40,48},{48,56},{1,9},{9,17},... | collective-permute-start | bytes 98312 | tf_op jit(solution)/shard_map/ppermute | solution.py:16
  223.8 4.7 %collective-permute-start.20 = (f32[1,8,1024]{2,1,0:T(8,128)S(1)}, f32[1,8,1024]{2,1,0:T(8,128)S(1)}, u32[]{:S(2)}, u32[]{:S(2)}) collective-permute-start(f32[1,8,1024]{2,1,0:T(8,128)S(1)} %get-tuple-element.108), channel_id=1, source_target_pairs={{8,0},{16,8},{24,16},{32,24},{40,32},{48,40},{56,48},{9,1},{17,9},... | collective-permute-start | bytes 98312 | tf_op jit(solution)/shard_map/ppermute | solution.py:17
  228.5 5.8 %collective-permute-start.23 = (f32[10,1,1024]{2,1,0:T(1,128)S(1)}, f32[10,1,1024]{2,1,0:T(1,128)S(1)}, u32[]{:S(2)}, u32[]{:S(2)}) collective-permute-start(f32[10,1,1024]{2,1,0:T(1,128)S(1)} %get-tuple-element.95), channel_id=1, source_target_pairs={{0,1},{1,2},{2,3},{3,4},{4,5},{5,6},{6,7},{8,9},{9,10},{10,11},{11... | collective-permute-start | bytes 122888 | tf_op jit(solution)/shard_map/ppermute | solution.py:16
  231.7 5.3 %collective-permute-start.22 = (f32[10,1,1024]{2,1,0:T(1,128)S(1)}, f32[10,1,1024]{2,1,0:T(1,128)S(1)}, u32[]{:S(2)}, u32[]{:S(2)}) collective-permute-start(f32[10,1,1024]{2,1,0:T(1,128)S(1)} %get-tuple-element.94), channel_id=1, source_target_pairs={{1,0},{2,1},{3,2},{4,3},{5,4},{6,5},{7,6},{9,8},{10,9},{11,10},{12... | collective-permute-start | bytes 122888 | tf_op jit(solution)/shard_map/ppermute | solution.py:17
  237.7 6.2 %collective-permute-start.25 = (f32[4,1,8,1024]{3,2,1,0:T(8,128)S(1)}, f32[4,1,8,1024]{3,2,1,0:T(8,128)S(1)}, u32[]{:S(2)}, u32[]{:S(2)}) collective-permute-start(f32[4,1,8,1024]{3,2,1,0:T(8,128)S(1)} %get-tuple-element.56), channel_id=1, source_target_pairs={{0,8},{8,16},{16,24},{24,32},{32,40},{40,48},{48,56},{1,9},{9,17},... | collective-permute-start | bytes 393224 | tf_op jit(solution)/shard_map/ppermute | solution.py:16
  242.0 6.2 %collective-permute-start.24 = (f32[4,1,8,1024]{3,2,1,0:T(8,128)S(1)}, f32[4,1,8,1024]{3,2,1,0:T(8,128)S(1)}, u32[]{:S(2)}, u32[]{:S(2)}) collective-permute-start(f32[4,1,8,1024]{3,2,1,0:T(8,128)S(1)} %get-tuple-element.57), channel_id=1, source_target_pairs={{8,0},{16,8},{24,16},{32,24},{40,32},{48,40},{56,48},{9,1},{17,9},... | collective-permute-start | bytes 393224 | tf_op jit(solution)/shard_map/ppermute | solution.py:17
  248.5 6.4 %collective-permute-start.27 = (f32[4,10,1,1024]{3,2,1,0:T(1,128)S(1)}, f32[4,10,1,1024]{3,2,1,0:T(1,128)S(1)}, u32[]{:S(2)}, u32[]{:S(2)}) collective-permute-start(f32[4,10,1,1024]{3,2,1,0:T(1,128)S(1)} %get-tuple-element.39), channel_id=1, source_target_pairs={{0,1},{1,2},{2,3},{3,4},{4,5},{5,6},{6,7},{8,9},{9,10},{10,11},{11... | collective-permute-start | bytes 491528 | tf_op jit(solution)/shard_map/ppermute | solution.py:16
  251.5 6.6 %collective-permute-start.26 = (f32[4,10,1,1024]{3,2,1,0:T(1,128)S(1)}, f32[4,10,1,1024]{3,2,1,0:T(1,128)S(1)}, u32[]{:S(2)}, u32[]{:S(2)}) collective-permute-start(f32[4,10,1,1024]{3,2,1,0:T(1,128)S(1)} %get-tuple-element.38), channel_id=1, source_target_pairs={{1,0},{2,1},{3,2},{4,3},{5,4},{6,5},{7,6},{9,8},{10,9},{11,10},{12... | collective-permute-start | bytes 491528 | tf_op jit(solution)/shard_map/ppermute | solution.py:17
  254.9 4.4 %copy-start.2 = (f32[8,8,1024]{2,1,0:T(8,128)S(1)}, f32[8,8,1024]{2,1,0:T(8,128)}, u32[]{:S(2)}) copy-start(f32[8,8,1024]{2,1,0:T(8,128)} %reshape.129) | copy-start | bytes 786436
  259.6 5.5 %collective-permute-start.33 = (f32[1,8,1024]{2,1,0:T(8,128)S(1)}, f32[1,8,1024]{2,1,0:T(8,128)S(1)}, u32[]{:S(2)}, u32[]{:S(2)}) collective-permute-start(f32[1,8,1024]{2,1,0:T(8,128)S(1)} %get-tuple-element.104), channel_id=1, source_target_pairs={{0,8},{8,16},{16,24},{24,32},{32,40},{40,48},{48,56},{1,9},{9,17},... | collective-permute-start | bytes 98312 | tf_op jit(solution)/shard_map/ppermute | solution.py:16
  263.6 4.7 %collective-permute-start.32 = (f32[1,8,1024]{2,1,0:T(8,128)S(1)}, f32[1,8,1024]{2,1,0:T(8,128)S(1)}, u32[]{:S(2)}, u32[]{:S(2)}) collective-permute-start(f32[1,8,1024]{2,1,0:T(8,128)S(1)} %get-tuple-element.105), channel_id=1, source_target_pairs={{8,0},{16,8},{24,16},{32,24},{40,32},{48,40},{56,48},{9,1},{17,9},... | collective-permute-start | bytes 98312 | tf_op jit(solution)/shard_map/ppermute | solution.py:17
  268.3 5.3 %collective-permute-start.35 = (f32[10,1,1024]{2,1,0:T(1,128)S(1)}, f32[10,1,1024]{2,1,0:T(1,128)S(1)}, u32[]{:S(2)}, u32[]{:S(2)}) collective-permute-start(f32[10,1,1024]{2,1,0:T(1,128)S(1)} %get-tuple-element.91), channel_id=1, source_target_pairs={{0,1},{1,2},{2,3},{3,4},{4,5},{5,6},{6,7},{8,9},{9,10},{10,11},{11... | collective-permute-start | bytes 122888 | tf_op jit(solution)/shard_map/ppermute | solution.py:16
  271.5 5.3 %collective-permute-start.34 = (f32[10,1,1024]{2,1,0:T(1,128)S(1)}, f32[10,1,1024]{2,1,0:T(1,128)S(1)}, u32[]{:S(2)}, u32[]{:S(2)}) collective-permute-start(f32[10,1,1024]{2,1,0:T(1,128)S(1)} %get-tuple-element.90), channel_id=1, source_target_pairs={{1,0},{2,1},{3,2},{4,3},{5,4},{6,5},{7,6},{9,8},{10,9},{11,10},{12... | collective-permute-start | bytes 122888 | tf_op jit(solution)/shard_map/ppermute | solution.py:17
  277.5 5.4 %collective-permute-start.37 = (f32[4,1,8,1024]{3,2,1,0:T(8,128)S(1)}, f32[4,1,8,1024]{3,2,1,0:T(8,128)S(1)}, u32[]{:S(2)}, u32[]{:S(2)}) collective-permute-start(f32[4,1,8,1024]{3,2,1,0:T(8,128)S(1)} %get-tuple-element.51), channel_id=1, source_target_pairs={{0,8},{8,16},{16,24},{24,32},{32,40},{40,48},{48,56},{1,9},{9,17},... | collective-permute-start | bytes 393224 | tf_op jit(solution)/shard_map/ppermute | solution.py:16
  281.0 5.7 %collective-permute-start.36 = (f32[4,1,8,1024]{3,2,1,0:T(8,128)S(1)}, f32[4,1,8,1024]{3,2,1,0:T(8,128)S(1)}, u32[]{:S(2)}, u32[]{:S(2)}) collective-permute-start(f32[4,1,8,1024]{3,2,1,0:T(8,128)S(1)} %get-tuple-element.52), channel_id=1, source_target_pairs={{8,0},{16,8},{24,16},{32,24},{40,32},{48,40},{56,48},{9,1},{17,9},... | collective-permute-start | bytes 393224 | tf_op jit(solution)/shard_map/ppermute | solution.py:17
  286.9 6.0 %collective-permute-start.39 = (f32[4,10,1,1024]{3,2,1,0:T(1,128)S(1)}, f32[4,10,1,1024]{3,2,1,0:T(1,128)S(1)}, u32[]{:S(2)}, u32[]{:S(2)}) collective-permute-start(f32[4,10,1,1024]{3,2,1,0:T(1,128)S(1)} %get-tuple-element.35), channel_id=1, source_target_pairs={{0,1},{1,2},{2,3},{3,4},{4,5},{5,6},{6,7},{8,9},{9,10},{10,11},{11... | collective-permute-start | bytes 491528 | tf_op jit(solution)/shard_map/ppermute | solution.py:16
  290.7 6.6 %collective-permute-start.38 = (f32[4,10,1,1024]{3,2,1,0:T(1,128)S(1)}, f32[4,10,1,1024]{3,2,1,0:T(1,128)S(1)}, u32[]{:S(2)}, u32[]{:S(2)}) collective-permute-start(f32[4,10,1,1024]{3,2,1,0:T(1,128)S(1)} %get-tuple-element.34), channel_id=1, source_target_pairs={{1,0},{2,1},{3,2},{4,3},{5,4},{6,5},{7,6},{9,8},{10,9},{11,10},{12... | collective-permute-start | bytes 491528 | tf_op jit(solution)/shard_map/ppermute | solution.py:17
  298.8 4.5 %collective-permute-start.45 = (f32[1,8,1024]{2,1,0:T(8,128)S(1)}, f32[1,8,1024]{2,1,0:T(8,128)S(1)}, u32[]{:S(2)}, u32[]{:S(2)}) collective-permute-start(f32[1,8,1024]{2,1,0:T(8,128)S(1)} %get-tuple-element.101), channel_id=1, source_target_pairs={{0,8},{8,16},{16,24},{24,32},{32,40},{40,48},{48,56},{1,9},{9,17},... | collective-permute-start | bytes 98312 | tf_op jit(solution)/shard_map/ppermute | solution.py:16
  301.6 4.7 %collective-permute-start.44 = (f32[1,8,1024]{2,1,0:T(8,128)S(1)}, f32[1,8,1024]{2,1,0:T(8,128)S(1)}, u32[]{:S(2)}, u32[]{:S(2)}) collective-permute-start(f32[1,8,1024]{2,1,0:T(8,128)S(1)} %get-tuple-element.102), channel_id=1, source_target_pairs={{8,0},{16,8},{24,16},{32,24},{40,32},{48,40},{56,48},{9,1},{17,9},... | collective-permute-start | bytes 98312 | tf_op jit(solution)/shard_map/ppermute | solution.py:17
  306.3 5.3 %collective-permute-start.47 = (f32[10,1,1024]{2,1,0:T(1,128)S(1)}, f32[10,1,1024]{2,1,0:T(1,128)S(1)}, u32[]{:S(2)}, u32[]{:S(2)}) collective-permute-start(f32[10,1,1024]{2,1,0:T(1,128)S(1)} %get-tuple-element.87), channel_id=1, source_target_pairs={{0,1},{1,2},{2,3},{3,4},{4,5},{5,6},{6,7},{8,9},{9,10},{10,11},{11... | collective-permute-start | bytes 122888 | tf_op jit(solution)/shard_map/ppermute | solution.py:16
  309.5 5.3 %collective-permute-start.46 = (f32[10,1,1024]{2,1,0:T(1,128)S(1)}, f32[10,1,1024]{2,1,0:T(1,128)S(1)}, u32[]{:S(2)}, u32[]{:S(2)}) collective-permute-start(f32[10,1,1024]{2,1,0:T(1,128)S(1)} %get-tuple-element.86), channel_id=1, source_target_pairs={{1,0},{2,1},{3,2},{4,3},{5,4},{6,5},{7,6},{9,8},{10,9},{11,10},{12... | collective-permute-start | bytes 122888 | tf_op jit(solution)/shard_map/ppermute | solution.py:17
Sparse Core Ops, SparseCore 0:
  317.7 19.9 reduce-scatter.1
